TPU v7x, 256 devices: a whole 4x4x8 slice. The times are simulated.
256 devices in a mesh: tiles: 32 (over z, x), sub: 8 (over y, core).
Axes of the slice: x: 4, y: 4, z: 8, core: 2. Of those that a mesh axis runs over, the one named last changes fastest.
Arguments:
- latents: float32 [196608, 512], P(('tiles', 'sub')), may hold values from -130 to 130
- conv_weight: float32 [512, 9, 512], P('tiles'), may hold values from -0.09375 to 0.09375
- conv_bias: float32 [512], replicated, may hold values from -4 to 4
- norm1_gain: float32 [512], replicated, may hold values from 0.5 to 1.5
- norm1_shift: float32 [512], replicated, may hold values from -3 to 3
- norm2_gain: float32 [512], replicated, may hold values from 0.5 to 1.5
- norm2_shift: float32 [512], replicated, may hold values from -3 to 3
- tile_counts: int32 [36], replicated, may hold values from 1 to 64, 768 in all
- widths: int32 [36], replicated, may hold values from 32 to 128, as said below
Outputs:
- activated: float32 [196608, 512], P(('tiles', 'sub'))
Inputs may be any that keep to these rules, and one draw needn't show every extreme that they name: `widths`: each width is 128, 64 or 32; some image has width 128 and some has width 128 / 4. `tile_counts`: they add up to 768; the largest is 64.
All inputs are finite; a program needn't handle non-finite values.
Results may differ from a plain program's by a relative error of at most 0.00014.
Values sent between devices are 32-bit elements; how exact they have to be, the bound alone decides.
A program may use at most 128 MiB of HBM per device.

v0:
```python
import jax
import jax.numpy as jnp
from jax import lax
from jax.sharding import PartitionSpec as P

GROUPS = 32
WMAX = 128
TILE = 256
epsilon = 1e-06
highest = lax.Precision.HIGHEST


def extended(cells, sides, width):
    for axis, dim in sides:
        count = lax.axis_size(axis)
        ends = count - 1
        head = lax.slice_in_dim(cells, 0, width, axis=dim)
        tail = lax.slice_in_dim(cells, cells.shape[dim] - width, cells.shape[dim], axis=dim)
        cells = jnp.concatenate(
            [
                lax.ppermute(tail, axis, [(i, (i + 1) % count) for i in range(ends)]),
                cells,
                lax.ppermute(head, axis, [((i + 1) % count, i) for i in range(ends)]),
            ],
            axis=dim,
        )
    return cells


def pixel_layout(tile_counts, widths, pixels_here):
    device = lax.axis_index("tiles") * lax.axis_size("sub") + lax.axis_index("sub")
    pixel_counts = tile_counts * TILE
    image_ends = jnp.cumsum(pixel_counts)
    image_starts = image_ends - pixel_counts
    position = device * pixels_here + jnp.arange(pixels_here, dtype=jnp.int32)
    member = (position[None, :] >= image_starts[:, None]) & (
        position[None, :] < image_ends[:, None]
    )

    def per_pixel(per_image):
        return jnp.sum(jnp.where(member, per_image[:, None], 0), axis=0)

    pixel_width = per_pixel(widths)
    offset = position - per_pixel(image_starts)
    row_index = offset // pixel_width
    column_index = offset - row_index * pixel_width
    pixel_height = per_pixel(pixel_counts) // pixel_width
    return (
        member.astype(jnp.float32),
        pixel_counts,
        row_index,
        column_index,
        pixel_width,
        pixel_height,
    )


def group_table(per_channel):
    return jnp.sum(per_channel.reshape(per_channel.shape[0], GROUPS, -1), axis=2)


def spread_rows(onehot, per_image):
    return lax.dot_general(
        onehot,
        per_image,
        (((0,), (0,)), ((), ())),
        precision=highest,
        preferred_element_type=jnp.float32,
    )


def normalize(values, norm_gain, norm_shift, onehot, pixel_counts):
    group_size = values.shape[1] // GROUPS
    entries = (pixel_counts * group_size).astype(jnp.float32)[:, None]
    firsts = jnp.dot(onehot, values, precision=highest, preferred_element_type=jnp.float32)
    group_total = lax.psum(group_table(firsts), ("tiles", "sub"))
    group_mean = group_total / entries
    centred = values - spread_rows(onehot, jnp.repeat(group_mean, group_size, axis=1))
    seconds = jnp.dot(
        onehot, centred * centred, precision=highest, preferred_element_type=jnp.float32
    )
    spread = lax.psum(group_table(seconds), ("tiles", "sub")) / entries
    inverse = spread_rows(onehot, jnp.repeat(lax.rsqrt(spread + epsilon), group_size, axis=1))
    return jax.nn.silu(centred * inverse * norm_gain + norm_shift)


def shards(
    latents,
    conv_weight,
    conv_bias,
    norm1_gain,
    norm1_shift,
    norm2_gain,
    norm2_shift,
    tile_counts,
    widths,
):
    pixels_here = latents.shape[0]
    channels = latents.shape[1]
    onehot, pixel_counts, row_index, column_index, pixel_width, pixel_height = pixel_layout(
        tile_counts, widths, pixels_here
    )
    first_act = normalize(latents, norm1_gain, norm1_shift, onehot, pixel_counts)
    padded = extended(first_act.T, ((("tiles", "sub"), 1),), WMAX + 1)
    anchor = jnp.arange(pixels_here, dtype=jnp.int32) + (WMAX + 1)
    sources = []
    validity = []
    for step_y in (-1, 0, 1):
        for step_x in (-1, 0, 1):
            inside = (row_index + step_y >= 0) & (row_index + step_y < pixel_height)
            inside = inside & (column_index + step_x >= 0) & (column_index + step_x < pixel_width)
            sources.append(jnp.where(inside, anchor + step_y * pixel_width + step_x, anchor))
            validity.append(inside.astype(jnp.float32))
    all_sources = jnp.concatenate(sources)
    all_masks = jnp.concatenate(validity)
    tapped = jnp.take(padded, all_sources, axis=1) * all_masks[None, :]
    zero_sum = jnp.zeros((pixels_here, channels), jnp.float32)
    running = zero_sum
    weight_piece = lax.all_gather(conv_weight, "tiles", axis=0, tiled=True)
    row_count = weight_piece.shape[0]
    block_width = min(row_count, 128)
    for block_start in range(0, row_count, block_width):
        block_rows = min(block_width, row_count - block_start)
        taps_block = lax.dynamic_slice_in_dim(tapped, block_start, block_rows, 0)
        taps_block = taps_block.reshape(block_rows, 9, pixels_here)
        weight_block = weight_piece[block_start : block_start + block_rows]
        running = running + jnp.einsum(
            "ktp,kto->po",
            taps_block,
            weight_block,
            precision=highest,
            preferred_element_type=jnp.float32,
        )
    hidden = running
    hidden = hidden + conv_bias
    return normalize(hidden, norm2_gain, norm2_shift, onehot, pixel_counts)


def solution(mesh):
    return jax.shard_map(
        shards,
        mesh=mesh,
        in_specs=(
            P(("tiles", "sub"), None),
            P("tiles", None, None),
            P(),
            P(),
            P(),
            P(),
            P(),
            P(),
            P(),
        ),
        out_specs=P(("tiles", "sub"), None),
        check_vma=False,
    )
```

profile of v0, /device:TPU:1, one launch (start us, length us, event | category | flops | bytes accessed | tf_op | source)
XLA Modules:
  0.0 427.4 jit_solution(8447993397408596706)
XLA Ops:
  6.5 0.0 copy-start.3
  6.5 0.0 all-gather.2.cloned.1.call-start
  6.5 0.7 all-gather.2.cloned.1.call-update
  7.3 0.7 broadcast_multiply_fusion
  7.9 0.1 copy.16
  8.0 0.1 reduce-window.8
  8.1 0.1 reduce
  8.2 0.7 fusion.25
  8.9 2.8 bitcast_reduce_fusion.3
  11.7 83.9 %psum.28 = f32[36,32]{0,1:T(8,128)S(1)} all-reduce(f32[36,32]{0,1:T(8,128)S(1)} %bitcast_reduce_fusion.3), channel_id=1, replica_groups=mesh['tiles'=32,'sub'=8] {'tiles','sub'}, use_global_device_ids=true, to_apply=%region_5.6 | all-reduce | flops 1152 | bytes 9216 | tf_op jit(solution)/shard_map/psum | solution.py:76
  95.6 0.0 copy-done.3
  95.6 0.9 convolution_subtract_fusion.1
  96.6 0.0 copy-start.7
  96.6 0.0 copy-start.8
  96.6 1.4 bitcast_reduce_fusion.2
  98.0 73.4 %psum.29 = f32[36,32]{0,1:T(8,128)S(1)} all-reduce(f32[36,32]{0,1:T(8,128)S(1)} %bitcast_reduce_fusion.2), channel_id=1, replica_groups=mesh['tiles'=32,'sub'=8] {'tiles','sub'}, use_global_device_ids=true, to_apply=%region_7.8 | all-reduce | flops 1152 | bytes 9216 | tf_op jit(solution)/shard_map/psum | solution.py:82
  171.5 0.0 copy-done.7
  171.5 0.0 copy-done.8
  171.5 0.0 copy-start.6
  171.5 1.3 multiply_bitcast_fusion.1
  172.8 0.0 copy-start.4
  172.8 1.1 copy-done.4
  174.0 3.2 collective-permute-start
  177.2 2.4 collective-permute-start.1
  179.6 0.0 copy-done.6
  179.6 0.1 select_reduce_fusion
  179.7 0.1 constant_dynamic-update-slice_fusion
  179.9 0.2 dynamic-update-slice
  180.1 0.2 dynamic-update-slice.1
  180.4 0.2 dynamic-update-slice.2
  180.6 0.1 constant_dynamic-update-slice_fusion.16
  180.8 0.2 dynamic-update-slice.3
  181.0 0.2 dynamic-update-slice.4
  181.3 0.2 dynamic-update-slice.5
  181.5 0.1 constant_dynamic-update-slice_fusion.13
  181.6 0.2 dynamic-update-slice.6
  181.9 0.2 dynamic-update-slice.7
  182.3 0.1 fusion.19
  182.4 0.0 collective-permute-done
  182.4 2.6 collective-permute-done.1
  185.0 4.5 %concatenate.54 = f32[512,1026]{0,1:T(8,128)S(1)} concatenate(f32[512,129]{0,1:T(8,128)S(1)} %collective-permute-done, f32[512,768]{0,1:T(8,128)} %copy-done.4, f32[512,129]{0,1:T(8,128)S(1)} %collective-permute-done.1), dimensions={1} | concatenate | bytes 4202496 | tf_op jit(solution)/shard_map/concatenate | solution.py:19
  189.5 18.6 %gather_fusion = f32[6912,512]{1,0:T(8,128)} fusion(f32[512,1026]{0,1:T(8,128)S(1)} %concatenate.54, s32[7168]{0:T(1024)S(1)} %pad_clamp_fusion), kind=kCustom, calls=%fused_computation | custom fusion | bytes 28339200 | tf_op jit(solution)/shard_map/jit(_take)/gather | solution.py:116
  208.1 11.6 %multiply_bitcast_fusion = f32[512,6912]{0,1:T(8,128)} fusion(f32[6912,512]{1,0:T(8,128)} %gather_fusion, f32[6912]{0:T(1024)S(1)} %concatenate.66, pred[6912]{0:T(1024)(128)(4,1)S(1)} %compare_and_fusion.1), kind=kLoop, calls=%fused_computation.1 | loop fusion | flops 7077888 | bytes 28346112 | tf_op jit(solution)/shard_map/mul | solution.py:116
  219.7 9.4 %fusion.35 = (f32[128,6912]{0,1:T(8,128)}, f32[128,6912]{0,1:T(8,128)}, f32[128,6912]{0,1:T(8,128)}, f32[128,6912]{0,1:T(8,128)S(1)}) fusion(f32[512,6912]{0,1:T(8,128)} %multiply_bitcast_fusion), kind=kLoop, calls=%fused_computation.106 | loop fusion | bytes 28311552 | tf_op jit(solution)/shard_map/dynamic_slice | solution.py:124
  229.1 9.2 %fusion = f32[768,512,1]{1,0,2:T(8,128)S(1)} fusion(f32[128,9,768]{0,2,1:T(8,128)} %bitcast.48, f32[512,9,512]{2,0,1:T(8,128)} %all-gather.2.cloned.1.call-done), kind=kOutput, calls=%fused_computation.2 | convolution fusion | flops 5435817984 | bytes 7471104 | tf_op jit(solution)/shard_map/ktp,kto->po/dot_general | solution.py:127
  238.2 0.0 copy-done
  238.2 8.0 %fusion.2 = f32[768,512,1]{1,0,2:T(8,128)S(1)} fusion(f32[128,9,768]{0,2,1:T(8,128)S(1)} %bitcast.47, f32[512,9,512]{2,0,1:T(8,128)} %all-gather.2.cloned.1.call-done), kind=kOutput, calls=%fused_computation.4 | convolution fusion | flops 5435817984 | bytes 7471104 | tf_op jit(solution)/shard_map/ktp,kto->po/dot_general | solution.py:127
  246.2 0.0 copy-done.2
  246.2 0.0 copy-start.1
  246.3 0.0 copy-start.5
  246.3 6.5 %fusion.4 = f32[768,512,1]{1,0,2:T(8,128)S(1)} fusion(f32[128,9,768]{0,2,1:T(8,128)S(1)} %bitcast.46, f32[512,9,512]{2,0,1:T(8,128)S(1)} %copy-done.2), kind=kOutput, calls=%fused_computation.6 | convolution fusion | flops 5435817984 | bytes 7471104 | tf_op jit(solution)/shard_map/ktp,kto->po/dot_general | solution.py:127
  252.8 0.0 copy-done.1
  252.8 0.0 copy-done.5
  252.8 6.4 %fusion.8 = f32[768,512]{1,0:T(8,128)S(1)} fusion(f32[768,512,1]{1,0,2:T(8,128)S(1)} %fusion, f32[768,512,1]{1,0,2:T(8,128)S(1)} %fusion.2, f32[768,512,1]{1,0,2:T(8,128)S(1)} %fusion.4, f32[128,9,768]{0,2,1:T(8,128)S(1)} %bitcast.49, f32[512,9,512]{2,0,1:T(8,128)S(1)} %copy-done.2, f32[512]{0:T(512)S(1)} %copy-done.5), kind=kOutput, calls=%fused_computation.11 | convolution fusion | flops 5437390848 | bytes 12191744 | tf_op jit(solution)/shard_map/ktp,kto->po/dot_general | solution.py:127
  259.2 1.4 bitcast_reduce_fusion.1
  260.6 82.0 %psum.30 = f32[36,32]{0,1:T(8,128)S(1)} all-reduce(f32[36,32]{0,1:T(8,128)S(1)} %bitcast_reduce_fusion.1), channel_id=1, replica_groups=mesh['tiles'=32,'sub'=8] {'tiles','sub'}, use_global_device_ids=true, to_apply=%region_9.10 | all-reduce | flops 1152 | bytes 9216 | tf_op jit(solution)/shard_map/psum | solution.py:76
  342.6 0.9 convolution_subtract_fusion
  343.6 0.0 copy-start.9
  343.6 0.0 copy-start.10
  343.6 1.4 bitcast_reduce_fusion
  345.0 72.8 %psum.31 = f32[36,32]{0,1:T(8,128)S(1)} all-reduce(f32[36,32]{0,1:T(8,128)S(1)} %bitcast_reduce_fusion), channel_id=1, replica_groups=mesh['tiles'=32,'sub'=8] {'tiles','sub'}, use_global_device_ids=true, to_apply=%region_11.12 | all-reduce | flops 1152 | bytes 9216 | tf_op jit(solution)/shard_map/psum | solution.py:82
  417.9 0.0 copy-done.9
  417.9 0.0 copy-done.10
  417.9 2.4 divide_multiply_fusion
  (37 shorter events, 0.4 us)
Async XLA Ops:
  6.5 89.1 %copy-start.3 = (f32[768,512]{1,0:T(8,128)S(1)}, f32[768,512]{1,0:T(8,128)}, u32[]{:S(2)}) copy-start(f32[768,512]{1,0:T(8,128)} %param.9) | copy-start | bytes 4718596
  6.5 222.5 %all-gather.2.cloned.1.call-start = ((), (), s32[]{:S(2)}) async-start(), calls=%async_computation | async-start | bytes 9732096 | tf_op jit(solution)/shard_map/all_gather | solution.py:119
  96.6 74.9 %copy-start.7 = (f32[512]{0:T(512)S(1)}, f32[512]{0:T(512)}, u32[]{:S(2)}) copy-start(f32[512]{0:T(512)} %param.13) | copy-start | bytes 6148
  96.6 74.9 %copy-start.8 = (f32[512]{0:T(512)S(1)}, f32[512]{0:T(512)}, u32[]{:S(2)}) copy-start(f32[512]{0:T(512)} %param.12) | copy-start | bytes 6148
  171.5 8.1 %copy-start.6 = (s32[36]{0:T(128)S(1)}, s32[36]{0:T(128)}, u32[]{:S(2)}) copy-start(s32[36]{0:T(128)} %param.17) | copy-start | bytes 436
  172.8 1.1 copy-start.4
  174.0 8.5 %collective-permute-start = (f32[512,129]{0,1:T(8,128)S(1)}, f32[512,129]{0,1:T(8,128)S(1)}, u32[]{:S(2)}, u32[]{:S(2)}) collective-permute-start(f32[512,129]{0,1:T(8,128)S(1)} %get-tuple-element.44), channel_id=1, source_target_pairs={{0,1},{1,2},{2,3},{3,4},{4,5},{5,6},{6,7},{7,8},{8,9},{9,10},{10,1... | collective-permute-start | bytes 792584 | tf_op jit(solution)/shard_map/ppermute | solution.py:21
  177.2 7.9 %collective-permute-start.1 = (f32[512,129]{0,1:T(8,128)S(1)}, f32[512,129]{0,1:T(8,128)S(1)}, u32[]{:S(2)}, u32[]{:S(2)}) collective-permute-start(f32[512,129]{0,1:T(8,128)S(1)} %get-tuple-element.43), channel_id=1, source_target_pairs={{1,0},{2,1},{3,2},{4,3},{5,4},{6,5},{7,6},{8,7},{9,8},{10,9},{11,1... | collective-permute-start | bytes 792584 | tf_op jit(solution)/shard_map/ppermute | solution.py:23
  229.1 9.2 %copy-start = (f32[128,6912]{0,1:T(8,128)S(1)}, f32[128,6912]{0,1:T(8,128)}, u32[]{:S(2)}) copy-start(f32[128,6912]{0,1:T(8,128)} %get-tuple-element.41) | copy-start | bytes 10616836
  229.1 17.2 %copy-start.2 = (f32[512,9,512]{2,0,1:T(8,128)S(1)}, f32[512,9,512]{2,0,1:T(8,128)}, u32[]{:S(2)}) copy-start(f32[512,9,512]{2,0,1:T(8,128)} %all-gather.2.cloned.1.call-done) | copy-start | bytes 28311556
  246.2 6.5 %copy-start.1 = (f32[128,6912]{0,1:T(8,128)S(1)}, f32[128,6912]{0,1:T(8,128)}, u32[]{:S(2)}) copy-start(f32[128,6912]{0,1:T(8,128)} %get-tuple-element.39) | copy-start | bytes 10616836
  246.3 6.5 %copy-start.5 = (f32[512]{0:T(512)S(1)}, f32[512]{0:T(512)}, u32[]{:S(2)}) copy-start(f32[512]{0:T(512)} %param.11) | copy-start | bytes 6148
  343.6 74.3 %copy-start.9 = (f32[512]{0:T(512)S(1)}, f32[512]{0:T(512)}, u32[]{:S(2)}) copy-start(f32[512]{0:T(512)} %param.15) | copy-start | bytes 6148
  343.6 74.3 %copy-start.10 = (f32[512]{0:T(512)S(1)}, f32[512]{0:T(512)}, u32[]{:S(2)}) copy-start(f32[512]{0:T(512)} %param.14) | copy-start | bytes 6148
Sparse Core Ops, SparseCore 0:
  9.9 107.2 all-gather.1
where the time goes:
time: 433 us; the launch traced here: 427 us
  blocking collectives  312 us (72%)
  matrix products  42.7 us (10%)
  local copies, waits for them, and re-layouts  35.8 us (8%)
  between operations  14 us (3%)
  other arithmetic  13.9 us (3%)
  starting transfers between devices  5.59 us (1%)
    psum x2, blocking collectives, normalize(): group_total = lax.psum(group_table(firsts), ('tiles', 'sub'))  166 us
    psum x2, blocking collectives, normalize(): spread = lax.psum(group_table(seconds), ('tiles', 'sub')) / entries  146 us
    dot_general x4, matrix products, shards(): jnp.einsum('ktp,kto->po', taps_block, weight_block, precision=highest, pr...  30 us
    gather x1, local copies, waits for them, and re-layouts, shards(): tapped = jnp.take(padded, all_sources, axis=1) * all_masks[None, :]  18.6 us
    mul x1, other arithmetic, shards(): tapped = jnp.take(padded, all_sources, axis=1) * all_masks[None, :]  11.6 us
    dynamic_slice x1, local copies, waits for them, and re-layouts, shards(): taps_block = lax.dynamic_slice_in_dim(tapped, block_start, block_rows, 0)  9.35 us
  transfers between devices with their start and end apart: 3, of which 1 were waited for; matrix products, arithmetic and copies ran while one was open for 13% of the time, Pallas kernels for 0%

commit v1 on v0

--- a/solution.py
+++ b/solution.py
@@ -73,7 +73,7 @@
     group_size = values.shape[1] // GROUPS
     entries = (pixel_counts * group_size).astype(jnp.float32)[:, None]
     firsts = jnp.dot(onehot, values, precision=highest, preferred_element_type=jnp.float32)
-    group_total = lax.psum(group_table(firsts), ("tiles", "sub"))
+    group_total = jnp.sum(lax.all_gather(group_table(firsts), ("tiles", "sub")), axis=0)
     group_mean = group_total / entries
     centred = values - spread_rows(onehot, jnp.repeat(group_mean, group_size, axis=1))
     seconds = jnp.dot(

time: 433 us -> 526 us (1.21)
  waiting for transfers between devices: 3.31 us -> 237 us
  blocking collectives: 312 us -> 153 us
  local copies, waits for them, and re-layouts: 35.8 us -> 44 us
  other arithmetic: 13.9 us -> 20.7 us
    all_gather x0 -> x2, waiting for transfers between devices: none -> 231 us  [normalize(): lax.all_gather(group_table(firsts), ('tiles', 'sub'))]
    psum x2 -> x0, blocking collectives: 166 us -> none  [normalize(): group_total = lax.psum(group_table(firsts), ('tiles', 'sub'))]
    unnamed x38, local copies, waits for them, and re-layouts: 3.19 us -> 11.4 us
    psum x2, blocking collectives: 146 us -> 153 us  [normalize(): spread = lax.psum(group_table(seconds), ('tiles', 'sub')) / entries]
  transfers between devices with their start and end apart: 3 -> 5, of which waited for: 1 -> 4; matrix products, arithmetic and copies ran while one was open for 13% -> 12% of each run, Pallas kernels for 0% -> 0%
where the time goes in v1:
time: 526 us; the launch traced here: 517 us
  waiting for transfers between devices  237 us (45%)
  blocking collectives  153 us (29%)
  matrix products  44.1 us (8%)
  local copies, waits for them, and re-layouts  44 us (8%)
  other arithmetic  20.7 us (4%)
  between operations  13.7 us (3%)
    all_gather x2, waiting for transfers between devices, normalize(): lax.all_gather(group_table(firsts), ('tiles', 'sub'))  231 us
    psum x2, blocking collectives, normalize(): spread = lax.psum(group_table(seconds), ('tiles', 'sub')) / entries  153 us
    dot_general x4, matrix products, shards(): jnp.einsum('ktp,kto->po', taps_block, weight_block, precision=highest, pr...  30 us
    gather x1, local copies, waits for them, and re-layouts, shards(): tapped = jnp.take(padded, all_sources, axis=1) * all_masks[None, :]  18.6 us
    mul x1, other arithmetic, shards(): tapped = jnp.take(padded, all_sources, axis=1) * all_masks[None, :]  12.1 us
    unnamed x38, local copies, waits for them, and re-layouts  11.4 us
  transfers between devices with their start and end apart: 5, of which 4 were waited for; matrix products, arithmetic and copies ran while one was open for 12% of the time, Pallas kernels for 0%

profile of v1, /device:TPU:1, one launch (start us, length us, event | category | flops | bytes accessed | tf_op | source)
XLA Modules:
  0.0 517.4 jit_solution(6417820005132604436)
XLA Ops:
  6.5 0.0 all-gather.10.cloned.1.call-start
  6.5 0.7 broadcast_multiply_fusion
  7.2 0.1 copy.21
  7.3 0.1 reduce-window.8
  7.4 0.1 reduce.2
  7.5 0.7 fusion.25
  8.2 3.5 bitcast_reduce_fusion.3
  11.6 0.0 all-gather.10.cloned.1.call-update
  11.6 0.0 all-gather.8.cloned.1.call-start
  11.7 0.7 all-gather.8.cloned.1.call-update
  12.4 0.0 all-gather.12.cloned.1.call-start
  12.5 0.1 select_reduce_fusion
  12.6 0.1 constant_dynamic-update-slice_fusion
  12.7 1.4 dynamic-update-slice
  14.2 1.4 dynamic-update-slice.1
  15.6 1.4 dynamic-update-slice.2
  17.0 0.1 constant_dynamic-update-slice_fusion.16
  17.2 1.4 dynamic-update-slice.3
  18.6 1.4 dynamic-update-slice.4
  20.0 1.4 dynamic-update-slice.5
  21.4 0.1 constant_dynamic-update-slice_fusion.13
  21.6 1.4 dynamic-update-slice.6
  23.0 1.4 dynamic-update-slice.7
  24.5 0.1 fusion.19
  24.6 0.6 constant_dynamic-update-slice_fusion.11
  25.2 106.5 %all-gather.10.cloned.1.call-done = f32[256,36,32]{1,2,0:T(8,128)} async-done(((f32[1,36,32]{1,2,0:T(8,128)}), f32[256,36,32]{1,2,0:T(8,128)}) %all-gather.10.cloned.1.call-update) | async-done | bytes 1179664 | tf_op jit(solution)/shard_map/all_gather | solution.py:76
  131.7 2.5 reduce_sum.85
  134.3 0.9 convolution_subtract_fusion.1
  135.2 0.0 copy-start.7
  135.2 0.0 copy-start.8
  135.2 1.4 bitcast_reduce_fusion.2
  136.7 77.5 %psum.14 = f32[36,32]{0,1:T(8,128)S(1)} all-reduce(f32[36,32]{0,1:T(8,128)S(1)} %bitcast_reduce_fusion.2), channel_id=1, replica_groups=mesh['tiles'=32,'sub'=8] {'tiles','sub'}, use_global_device_ids=true, to_apply=%region_7.8 | all-reduce | flops 1152 | bytes 9216 | tf_op jit(solution)/shard_map/psum | solution.py:82
  214.3 0.0 copy-done.7
  214.3 0.0 copy-done.8
  214.3 1.3 multiply_bitcast_fusion.1
  215.6 0.0 copy-start.4
  215.6 3.2 collective-permute-start
  218.8 1.9 collective-permute-start.1
  220.7 0.7 concatenate.66
  221.5 0.8 collective-permute-done
  222.3 4.8 collective-permute-done.1
  227.1 4.5 concatenate.54
  231.6 18.6 %gather_fusion = f32[6912,512]{1,0:T(8,128)} fusion(f32[512,1026]{0,1:T(8,128)S(1)} %concatenate.54, s32[7168]{0:T(1024)S(1)} %pad_clamp_fusion), kind=kCustom, calls=%fused_computation | custom fusion | bytes 28339200 | tf_op jit(solution)/shard_map/jit(_take)/gather | solution.py:116
  250.1 12.1 %multiply_bitcast_fusion = f32[512,6912]{0,1:T(8,128)} fusion(f32[6912,512]{1,0:T(8,128)} %gather_fusion, f32[6912]{0:T(1024)S(1)} %concatenate.66, pred[6912]{0:T(1024)(128)(4,1)S(1)} %compare_and_fusion.1), kind=kLoop, calls=%fused_computation.1 | loop fusion | flops 7077888 | bytes 28346112 | tf_op jit(solution)/shard_map/mul | solution.py:116
  262.2 9.4 %fusion.35 = (f32[128,6912]{0,1:T(8,128)}, f32[128,6912]{0,1:T(8,128)}, f32[128,6912]{0,1:T(8,128)}, f32[128,6912]{0,1:T(8,128)S(1)}) fusion(f32[512,6912]{0,1:T(8,128)} %multiply_bitcast_fusion), kind=kLoop, calls=%fused_computation.106 | loop fusion | bytes 28311552 | tf_op jit(solution)/shard_map/dynamic_slice | solution.py:124
  271.6 9.2 %fusion = f32[768,512,1]{1,0,2:T(8,128)S(1)} fusion(f32[128,9,768]{0,2,1:T(8,128)} %bitcast.50, f32[512,9,512]{2,0,1:T(8,128)} %all-gather.8.cloned.1.call-done), kind=kOutput, calls=%fused_computation.2 | convolution fusion | flops 5435817984 | bytes 7471104 | tf_op jit(solution)/shard_map/ktp,kto->po/dot_general | solution.py:127
  280.7 8.0 %fusion.2 = f32[768,512,1]{1,0,2:T(8,128)S(1)} fusion(f32[128,9,768]{0,2,1:T(8,128)S(1)} %bitcast.49, f32[512,9,512]{2,0,1:T(8,128)} %all-gather.8.cloned.1.call-done), kind=kOutput, calls=%fused_computation.4 | convolution fusion | flops 5435817984 | bytes 7471104 | tf_op jit(solution)/shard_map/ktp,kto->po/dot_general | solution.py:127
  288.7 0.0 copy-done.2
  288.7 0.0 copy-start.1
  288.7 0.0 copy-start.5
  288.8 6.5 %fusion.4 = f32[768,512,1]{1,0,2:T(8,128)S(1)} fusion(f32[128,9,768]{0,2,1:T(8,128)S(1)} %bitcast.48, f32[512,9,512]{2,0,1:T(8,128)S(1)} %copy-done.2), kind=kOutput, calls=%fused_computation.6 | convolution fusion | flops 5435817984 | bytes 7471104 | tf_op jit(solution)/shard_map/ktp,kto->po/dot_general | solution.py:127
  295.2 0.0 copy-done.1
  295.2 0.0 copy-done.5
  295.3 6.4 %fusion.8 = f32[768,512]{1,0:T(8,128)S(1)} fusion(f32[768,512,1]{1,0,2:T(8,128)S(1)} %fusion, f32[768,512,1]{1,0,2:T(8,128)S(1)} %fusion.2, f32[768,512,1]{1,0,2:T(8,128)S(1)} %fusion.4, f32[128,9,768]{0,2,1:T(8,128)S(1)} %bitcast.51, f32[512,9,512]{2,0,1:T(8,128)S(1)} %copy-done.2, f32[512]{0:T(512)S(1)} %copy-done.5), kind=kOutput, calls=%fused_computation.11 | convolution fusion | flops 5437390848 | bytes 12191744 | tf_op jit(solution)/shard_map/ktp,kto->po/dot_general | solution.py:127
  301.7 2.1 bitcast_reduce_fusion.1
  303.7 0.0 all-gather.12.cloned.1.call-update
  303.7 124.0 %all-gather.12.cloned.1.call-done = f32[256,36,32]{1,2,0:T(8,128)} async-done(((f32[1,36,32]{1,2,0:T(8,128)}), f32[256,36,32]{1,2,0:T(8,128)}) %all-gather.12.cloned.1.call-update) | async-done | bytes 1179664 | tf_op jit(solution)/shard_map/all_gather | solution.py:76
  427.8 2.5 reduce_sum.88
  430.3 1.1 convolution_subtract_fusion
  431.5 0.0 copy-start.9
  431.5 0.0 copy-start.10
  431.5 1.4 bitcast_reduce_fusion
  433.0 75.2 %psum.15 = f32[36,32]{0,1:T(8,128)S(1)} all-reduce(f32[36,32]{0,1:T(8,128)S(1)} %bitcast_reduce_fusion), channel_id=1, replica_groups=mesh['tiles'=32,'sub'=8] {'tiles','sub'}, use_global_device_ids=true, to_apply=%region_11.12 | all-reduce | flops 1152 | bytes 9216 | tf_op jit(solution)/shard_map/psum | solution.py:82
  508.2 2.4 divide_multiply_fusion
  (43 shorter events, 0.4 us)
Async XLA Ops:
  6.5 5.9 %copy-start.6 = (s32[36]{0:T(128)S(1)}, s32[36]{0:T(128)}, u32[]{:S(2)}) copy-start(s32[36]{0:T(128)} %param.17) | copy-start | bytes 436
  6.5 125.2 %all-gather.10.cloned.1.call-start = ((), (), s32[]{:S(2)}) async-start(), calls=%async_computation.1 | async-start | bytes 4210688 | tf_op jit(solution)/shard_map/all_gather | solution.py:76
  11.6 259.9 %all-gather.8.cloned.1.call-start = ((), (), s32[]{:S(2)}) async-start(), calls=%async_computation | async-start | bytes 9732096 | tf_op jit(solution)/shard_map/all_gather | solution.py:119
  12.4 415.4 %all-gather.12.cloned.1.call-start = ((), (), s32[]{:S(2)}) async-start(), calls=%async_computation.2 | async-start | bytes 4210688 | tf_op jit(solution)/shard_map/all_gather | solution.py:76
  25.2 109.1 %copy-start.3 = (f32[768,512]{1,0:T(8,128)S(1)}, f32[768,512]{1,0:T(8,128)}, u32[]{:S(2)}) copy-start(f32[768,512]{1,0:T(8,128)} %param.9) | copy-start | bytes 4718596
  135.2 79.1 %copy-start.7 = (f32[512]{0:T(512)S(1)}, f32[512]{0:T(512)}, u32[]{:S(2)}) copy-start(f32[512]{0:T(512)} %param.13) | copy-start | bytes 6148
  135.2 79.1 %copy-start.8 = (f32[512]{0:T(512)S(1)}, f32[512]{0:T(512)}, u32[]{:S(2)}) copy-start(f32[512]{0:T(512)} %param.12) | copy-start | bytes 6148
  215.6 6.7 %copy-start.4 = (f32[512,768]{0,1:T(8,128)}, f32[512,768]{0,1:T(8,128)S(1)}, u32[]{:S(2)}) copy-start(f32[512,768]{0,1:T(8,128)S(1)} %multiply_bitcast_fusion.1) | copy-start | bytes 4718596
  215.6 6.6 %collective-permute-start = (f32[512,129]{0,1:T(8,128)S(1)}, f32[512,129]{0,1:T(8,128)S(1)}, u32[]{:S(2)}, u32[]{:S(2)}) collective-permute-start(f32[512,129]{0,1:T(8,128)S(1)} %get-tuple-element.44), channel_id=1, source_target_pairs={{0,1},{1,2},{2,3},{3,4},{4,5},{5,6},{6,7},{7,8},{8,9},{9,10},{10,1... | collective-permute-start | bytes 792584 | tf_op jit(solution)/shard_map/ppermute | solution.py:21
  218.8 8.3 %collective-permute-start.1 = (f32[512,129]{0,1:T(8,128)S(1)}, f32[512,129]{0,1:T(8,128)S(1)}, u32[]{:S(2)}, u32[]{:S(2)}) collective-permute-start(f32[512,129]{0,1:T(8,128)S(1)} %get-tuple-element.43), channel_id=1, source_target_pairs={{1,0},{2,1},{3,2},{4,3},{5,4},{6,5},{7,6},{8,7},{9,8},{10,9},{11,1... | collective-permute-start | bytes 792584 | tf_op jit(solution)/shard_map/ppermute | solution.py:23
  271.5 9.2 %copy-start = (f32[128,6912]{0,1:T(8,128)S(1)}, f32[128,6912]{0,1:T(8,128)}, u32[]{:S(2)}) copy-start(f32[128,6912]{0,1:T(8,128)} %get-tuple-element.41) | copy-start | bytes 10616836
  271.6 17.2 %copy-start.2 = (f32[512,9,512]{2,0,1:T(8,128)S(1)}, f32[512,9,512]{2,0,1:T(8,128)}, u32[]{:S(2)}) copy-start(f32[512,9,512]{2,0,1:T(8,128)} %all-gather.8.cloned.1.call-done) | copy-start | bytes 28311556
  288.7 6.5 %copy-start.1 = (f32[128,6912]{0,1:T(8,128)S(1)}, f32[128,6912]{0,1:T(8,128)}, u32[]{:S(2)}) copy-start(f32[128,6912]{0,1:T(8,128)} %get-tuple-element.39) | copy-start | bytes 10616836
  288.7 6.5 %copy-start.5 = (f32[512]{0:T(512)S(1)}, f32[512]{0:T(512)}, u32[]{:S(2)}) copy-start(f32[512]{0:T(512)} %param.11) | copy-start | bytes 6148
  431.5 76.7 %copy-start.9 = (f32[512]{0:T(512)S(1)}, f32[512]{0:T(512)}, u32[]{:S(2)}) copy-start(f32[512]{0:T(512)} %param.15) | copy-start | bytes 6148
  431.5 76.7 %copy-start.10 = (f32[512]{0:T(512)S(1)}, f32[512]{0:T(512)}, u32[]{:S(2)}) copy-start(f32[512]{0:T(512)} %param.14) | copy-start | bytes 6148
Sparse Core Ops, SparseCore 0:
  11.8 119.9 all-gather.9
  134.3 100.1 all-gather.7
  303.9 123.8 all-gather.11
